TPU v7x, 32 devices: a whole 2x2x4 slice. The times are simulated.
32 devices in a mesh: term: 8 (over y, x, core), topic: 4 (over z).
Axes of the slice: x: 2, y: 2, z: 4, core: 2. Of those that a mesh axis runs over, the one named last changes fastest.
Arguments:
- factor: bfloat16 [65536, 512], P('term', 'topic'), may hold values from 1e-06 to 0.05, as said below
- tile_values: bfloat16 [65536, 128], P('term'), may hold values from 0.049804688 to 1
- tile_docs: int32 [8, 128], P('term'), may hold values from 0 to 127, as said below
- codes: float32 [512, 128], P('topic', 'term'), may hold values from 0.1 to 2
- gram_stat: float32 [512, 512], P('topic', 'term'), may hold values from 0 to 4
- data_stat: float32 [65536, 512], P('term', 'topic'), may hold values from 0 to 0.4
Outputs:
- codes_out: float32 [512, 128], P('topic', 'term')
- gram_new: float32 [512, 512], P('topic', 'term')
- data_new: float32 [65536, 512], P('term', 'topic')
Inputs may be any that keep to these rules, and one draw needn't show every extreme that they name: `tile_docs`: each row lists 128 different document numbers. `factor`: positive entries.
All inputs are finite; a program needn't handle non-finite values.
Results may differ from a plain program's by a relative error of at most 0.0003.
Values may be sent and summed in bfloat16 or wider, within the bound.
No kernel may reach another device: no remote copies, remote signals or barrier semaphores. Data moves between devices by JAX's collectives and lax.ppermute only.
A program may use at most 128 MiB of HBM per device.

v0:
```python
import functools
import jax
import jax.numpy as jnp
from jax import lax
from jax.experimental import pallas as pl
from jax.experimental.pallas import tpu as pltpu
from jax.sharding import PartitionSpec as P


ITERS = 3
EPSILON = 1e-06
DECAY = 0.5
ROW_CHUNKS = 8
UPDATE_GRANT = 53 * 2**20


VMEM = pl.BlockSpec(memory_space=pltpu.VMEM)
ANY = pl.BlockSpec(memory_space=pl.ANY)
HBM = pl.BlockSpec(memory_space=pltpu.HBM)
SMEM = pl.BlockSpec(memory_space=pltpu.SMEM)


def contract_rows(left, right):
    return lax.dot_general(
        left, right, (((0,), (0,)), ((), ())), preferred_element_type=jnp.float32
    )


def swap(value, axis, offset):
    return lax.ppermute(
        value, axis, [(i, i ^ offset) for i in range(lax.axis_size(axis))]
    )


def gather_term(piece, chips):
    near = [piece] + [swap(piece, "term", 2 * k) for k in range(1, chips)]
    far = [swap(value, "term", 1) for value in near]
    return [value for pair in zip(near, far) for value in pair]


def split(value):
    high = value.astype(jnp.bfloat16)
    return high, (value - high.astype(jnp.float32)).astype(jnp.bfloat16)


def pairs_of(count):
    return [(i, j) for i in range(count) for j in range(i + 1, count)]


def gram_kernel(groups, place, factor, *rest):
    arrived = rest[: groups - 1]
    out, rows, block, sem = rest[groups - 1 :]
    z = place[0]
    share = rows.shape[1]
    copies = [
        pltpu.make_async_copy(
            factor.at[pl.ds(pl.multiple_of(z * share, share), share)], rows.at[z], sem.at[0]
        )
    ]
    for k in range(1, groups):
        copies.append(pltpu.make_async_copy(arrived[k - 1], rows.at[z ^ k], sem.at[k]))
    for copy in copies:
        copy.start()
    for copy in copies:
        copy.wait()
    devices, _, piece, _ = out.shape
    for index, (i, j) in enumerate(pairs_of(groups)):
        block[...] = contract_rows(rows[i], rows[j])
        for device in range(devices):
            out[device, index] = block[device * piece : (device + 1) * piece, :]


def gram_blocks(place, factor, arrived, groups, devices):
    share, width = arrived[0].shape
    shape = (devices, groups * (groups - 1) // 2, width // devices, width)
    scratch = groups * share * width * 2 + groups * groups * width * width * 2
    return pl.pallas_call(
        functools.partial(gram_kernel, groups),
        out_shape=jax.ShapeDtypeStruct(shape, jnp.float32),
        in_specs=[SMEM, ANY] + [ANY] * (groups - 1),
        out_specs=VMEM,
        scratch_shapes=[
            pltpu.VMEM((groups, share, width), jnp.bfloat16),
            pltpu.VMEM((width, width), jnp.float32),
            pltpu.SemaphoreType.DMA((groups,)),
        ],
        compiler_params=pltpu.CompilerParams(vmem_limit_bytes=2 * scratch + 8 * 2**20),
        name="gram_blocks",
    )(place, factor, *arrived)


def assemble_kernel(devices, groups, place, *refs):
    pieces, outs = refs[:devices], refs[devices:]
    z, term = place[0], place[1]
    for k in range(devices):
        start = 0
        for out in outs:
            size = out.shape[1] // devices
            row = pl.multiple_of((term ^ k) * size, size)
            for r in range(groups):
                out[z ^ r, pl.ds(row, size), :] = pieces[k][r, start : start + size, :]
            start += size


def assemble(place, pieces, documents):
    groups, _, width = pieces[0].shape
    devices = len(pieces)
    return pl.pallas_call(
        functools.partial(assemble_kernel, devices, groups),
        out_shape=[
            jax.ShapeDtypeStruct((groups, rows, width), jnp.float32)
            for rows in (documents, documents, width)
        ],
        in_specs=[SMEM] + [VMEM] * devices,
        out_specs=[VMEM] * 3,
        compiler_params=pltpu.CompilerParams(
            vmem_limit_bytes=16 * groups * (2 * documents + width) * width + 4 * 2**20
        ),
        name="assemble",
    )(place, *pieces)


def dot3(left, right):
    dot = functools.partial(jnp.dot, preferred_element_type=jnp.float32)
    return dot(left[0], right[0]) + (dot(left[0], right[1]) + dot(left[1], right[0]))


def update_kernel(devices, groups, place, docs, codes, data, diagonal, stat, old, tiles, *rest):
    pieces = rest[:devices]
    codes_out, gram_new, data_new = rest[devices : devices + 3]
    high, low, cur, blocks, tile_buf, old_buf, piece_sem, tile_sem, old_sem, new_sem = rest[
        devices + 3 :
    ]
    z, term = place[0], place[1]
    width, documents = codes.shape[2], codes.shape[1]
    piece = width // devices
    landings = []
    for k in range(devices):
        row = pl.multiple_of((term ^ k) * piece, piece)
        copy = pltpu.make_async_copy(
            pieces[k], blocks.at[:, pl.ds(row, piece), :], piece_sem.at[k]
        )
        copy.start()
        landings.append(copy)
    rows = old.shape[0] // ROW_CHUNKS
    tile_in, old_in = [], []
    for chunk in range(ROW_CHUNKS):
        span = pl.ds(chunk * rows, rows)
        copy = pltpu.make_async_copy(tiles.at[span], tile_buf.at[span], tile_sem.at[chunk])
        copy.start()
        tile_in.append(copy)
        copy = pltpu.make_async_copy(old.at[span], old_buf.at[span], old_sem.at[chunk])
        copy.start()
        old_in.append(copy)
    for copy in landings:
        copy.wait()

    def place_block(i, j, value):
        at = (pl.ds(i * width, width), pl.ds(j * width, width))
        high[at], low[at] = split(value)

    for i in range(groups):
        place_block(i, i, diagonal[i])
        cur[:, pl.ds(i * width, width)] = codes[i]
    for index, (i, j) in enumerate(pairs_of(groups)):
        value = blocks[index]
        place_block(i, j, value)
        place_block(j, i, value.T)

    for _ in range(ITERS):
        applied = dot3(split(cur[...]), (high[...], low[...]))
        for i in range(groups):
            at = pl.ds(i * width, width)
            cur[:, at] = cur[:, at] * data[i] / (applied[:, i * width : (i + 1) * width] + EPSILON)

    own = cur[:, pl.ds(pl.multiple_of(z * width, width), width)]
    own_pair = split(own / documents)
    onehot = (
        lax.broadcasted_iota(jnp.int32, (documents, docs.shape[1]), 0) == docs[...]
    ).astype(jnp.bfloat16)
    picked = [contract_rows(onehot, value).astype(jnp.bfloat16) for value in own_pair]
    stacked = jnp.concatenate(picked, axis=0)
    stores = []
    for chunk in range(ROW_CHUNKS):
        span = pl.ds(chunk * rows, rows)
        tile_in[chunk].wait()
        old_in[chunk].wait()
        tile = tile_buf[span, :]
        old_buf[span, :] = DECAY * old_buf[span, :] + jnp.dot(
            jnp.concatenate([tile, tile], axis=1), stacked, preferred_element_type=jnp.float32
        )
        copy = pltpu.make_async_copy(old_buf.at[span], data_new.at[span], new_sem.at[chunk])
        copy.start()
        stores.append(copy)

    share = documents // devices
    codes_out[...] = cur[
        pl.ds(pl.multiple_of(term * share, share), share),
        pl.ds(pl.multiple_of(z * width, width), width),
    ]
    columns = stat.shape[0]
    first = term * columns
    group = first // width
    other = split(cur[:, pl.ds(pl.multiple_of(group * width, width), width)])
    blocks[0] = contract_rows(other[0], own_pair[0]) + (
        contract_rows(other[0], own_pair[1]) + contract_rows(other[1], own_pair[0])
    )
    offset = pl.multiple_of(first - group * width, columns)
    gram_new[...] = DECAY * stat[...] + blocks[0, pl.ds(offset, columns), :]
    for copy in stores:
        copy.wait()


def update(place, docs, codes, data, diagonal, stat, old, tiles, pieces):
    groups, documents, width = codes.shape
    topics = groups * width
    devices = len(pieces)
    return pl.pallas_call(
        functools.partial(update_kernel, devices, groups),
        out_shape=[
            jax.ShapeDtypeStruct((documents // devices, width), jnp.float32),
            jax.ShapeDtypeStruct(stat.shape, jnp.float32),
            jax.ShapeDtypeStruct(old.shape, jnp.float32),
        ],
        in_specs=[SMEM, VMEM, VMEM, VMEM, VMEM, VMEM, HBM, HBM] + [ANY] * devices,
        out_specs=[VMEM, VMEM, HBM],
        scratch_shapes=[
            pltpu.VMEM((topics, topics), jnp.bfloat16),
            pltpu.VMEM((topics, topics), jnp.bfloat16),
            pltpu.VMEM((documents, topics), jnp.float32),
            pltpu.VMEM((groups * (groups - 1) // 2, width, width), jnp.float32),
            pltpu.VMEM(tiles.shape, tiles.dtype),
            pltpu.VMEM(old.shape, old.dtype),
            pltpu.SemaphoreType.DMA((devices,)),
            pltpu.SemaphoreType.DMA((ROW_CHUNKS,)),
            pltpu.SemaphoreType.DMA((ROW_CHUNKS,)),
            pltpu.SemaphoreType.DMA((ROW_CHUNKS,)),
        ],
        compiler_params=pltpu.CompilerParams(
            vmem_limit_bytes=UPDATE_GRANT
        ),
        name="update",
    )(place, docs, codes, data, diagonal, stat, old, tiles, *pieces)


def exchange_order(groups):
    return [k for k in range(2, groups, 2)] + [k for k in range(1, groups, 2)]


def per_device(factor, tile_values, tile_docs, codes, gram_stat, data_stat):
    devices, groups = lax.axis_size("term"), lax.axis_size("topic")
    term, z = lax.axis_index("term"), lax.axis_index("topic")
    chips = devices // 2
    rows, width = factor.shape
    share = rows // groups
    mine = codes.shape[1]
    documents = mine * devices
    piece = width // devices
    place = jnp.stack([z, term]).astype(jnp.int32)

    order = exchange_order(groups)
    first, others = order[0], order[1:]

    def exchange(k, source):
        block = lax.dynamic_slice_in_dim(source, (z ^ k) * share, share, 0)
        return swap(block, "topic", k)

    arrived = {first: exchange(first, factor)}

    onehot = (
        jnp.arange(documents, dtype=jnp.int32)[:, None] == tile_docs[0][None, :]
    ).astype(jnp.float32)
    by_tile = contract_rows(tile_values, factor)
    data_part = jnp.dot(
        onehot, by_tile, precision=lax.Precision.HIGHEST, preferred_element_type=jnp.float32
    )
    diagonal_part = contract_rows(factor, factor)
    early = jnp.concatenate(
        [data_part.reshape(devices, mine, width), diagonal_part.reshape(devices, piece, width)],
        axis=1,
    )
    early = jnp.sum(lax.all_to_all(early, "term", 0, 0, tiled=True), axis=0)
    early = jnp.concatenate([codes.T, early], axis=0)
    by_group = [early] + [swap(early, "topic", k) for k in range(1, groups)]
    later, early = lax.optimization_barrier((factor, early))
    for k in others:
        arrived[k] = exchange(k, later)
    codes_all, data_all, diagonal_all = assemble(
        place, gather_term(jnp.stack(by_group), chips), documents
    )
    arrived, codes_all, data_all, diagonal_all = lax.optimization_barrier(
        (arrived, codes_all, data_all, diagonal_all)
    )
    blocks = gram_blocks(place, factor, [arrived[k] for k in range(1, groups)], groups, devices)
    total = jnp.sum(lax.all_to_all(blocks, "term", 0, 0, tiled=True), axis=0)
    whole = total
    for part in [swap(total, "topic", k) for k in order]:
        whole = whole + part
    pieces = gather_term(whole, chips)
    codes_out, gram_new, data_new = update(
        place, tile_docs, codes_all, data_all, diagonal_all, gram_stat.T, data_stat, tile_values, pieces
    )
    return codes_out.T, gram_new.T, data_new


def solution(mesh):
    placed = (
        P("term", "topic"),
        P("term", None),
        P("term", None),
        P("topic", "term"),
        P("topic", "term"),
        P("term", "topic"),
    )
    return jax.shard_map(
        per_device,
        mesh=mesh,
        in_specs=placed,
        out_specs=(P("topic", "term"), P("topic", "term"), P("term", "topic")),
        check_vma=False,
    )
```

profile of v0, /device:TPU:0, one launch (start us, length us, event | category | flops | bytes accessed | tf_op | source)
XLA Modules:
  0.0 110.1 jit_solution(10149151607798916898)
XLA Ops:
  0.7 3.1 %fusion.4 = f32[128,128]{1,0:T(8,128)S(1)} fusion(bf16[8192,128]{1,0:T(8,128)(2,1)} %factor.1), kind=kOutput, calls=%fused_computation.13 | convolution fusion | flops 268435456 | bytes 2162688 | tf_op jit(solution)/shard_map/dot_general | solution.py:24
  3.8 0.3 copy-done.12
  4.1 0.7 fusion.3
  5.1 0.7 pad_maximum_fusion
  5.7 5.2 %all-to-all-start = ((f32[8,32,128]{2,1,0:T(8,128)}), f32[8,32,128]{2,1,0:T(8,128)S(1)}, u32[]{:S(2)}, u32[]{:S(2)}) async-start(f32[8,32,128]{2,1,0:T(8,128)} %pad_maximum_fusion), calls=%async_computation | async-start | bytes 262144 | tf_op jit(solution)/shard_map/all_to_all | solution.py:282
  10.9 0.8 constant_dynamic-slice_fusion.1
  11.8 2.6 %collective-permute-start.1 = (bf16[2048,128]{1,0:T(8,128)(2,1)}, bf16[2048,128]{1,0:T(8,128)(2,1)S(1)}, u32[]{:S(2)}, u32[]{:S(2)}) collective-permute-start(bf16[2048,128]{1,0:T(8,128)(2,1)} %constant_dynamic-slice_fusion.1), channel_id=1, source_target_pairs={{0,2},{1,3},{2,0},{3,1},{4,6},{5,7},{6,4},{7,5},{8,10},{9,11},{10,... | collective-permute-start | bytes 1572872 | tf_op jit(solution)/shard_map/ppermute | solution.py:30
  14.3 2.1 %all-to-all-done = f32[8,32,128]{2,1,0:T(8,128)S(1)} async-done(((f32[8,32,128]{2,1,0:T(8,128)}), f32[8,32,128]{2,1,0:T(8,128)S(1)}, u32[]{:S(2)}, u32[]{:S(2)}) %all-to-all-start) | async-done | bytes 131104 | tf_op jit(solution)/shard_map/all_to_all | solution.py:282
  16.5 2.7 %collective-permute-start.4 = (f32[48,128]{1,0:T(8,128)S(1)}, f32[48,128]{1,0:T(8,128)S(1)}, u32[]{:S(2)}, u32[]{:S(2)}) collective-permute-start(f32[48,128]{1,0:T(8,128)S(1)} %get-tuple-element.32), channel_id=1, source_target_pairs={{0,2},{1,3},{2,0},{3,1},{4,6},{5,7},{6,4},{7,5},{8,10},{9,11},{10,... | collective-permute-start | bytes 73736 | tf_op jit(solution)/shard_map/ppermute | solution.py:30
  19.1 1.6 %collective-permute-start.3 = (f32[48,128]{1,0:T(8,128)S(1)}, f32[48,128]{1,0:T(8,128)S(1)}, u32[]{:S(2)}, u32[]{:S(2)}) collective-permute-start(f32[48,128]{1,0:T(8,128)S(1)} %get-tuple-element.32), channel_id=1, source_target_pairs={{0,1},{1,0},{2,3},{3,2},{4,5},{5,4},{6,7},{7,6},{8,9},{9,8},{10,11... | collective-permute-start | bytes 73736 | tf_op jit(solution)/shard_map/ppermute | solution.py:30
  20.9 1.0 constant_dynamic-slice_fusion
  22.0 3.6 %collective-permute-start.2 = (bf16[2048,128]{1,0:T(8,128)(2,1)}, bf16[2048,128]{1,0:T(8,128)(2,1)S(1)}, u32[]{:S(2)}, u32[]{:S(2)}) collective-permute-start(bf16[2048,128]{1,0:T(8,128)(2,1)} %get-tuple-element.29), channel_id=1, source_target_pairs={{0,3},{1,2},{2,1},{3,0},{4,7},{5,6},{6,5},{7,4},{8,11},{9,10},{10,... | collective-permute-start | bytes 1572872 | tf_op jit(solution)/shard_map/ppermute | solution.py:30
  25.6 26.1 %collective-permute-done.4 = f32[48,128]{1,0:T(8,128)S(1)} collective-permute-done((f32[48,128]{1,0:T(8,128)S(1)}, f32[48,128]{1,0:T(8,128)S(1)}, u32[]{:S(2)}, u32[]{:S(2)}) %collective-permute-start.4) | collective-permute-done | bytes 24608 | tf_op jit(solution)/shard_map/ppermute | solution.py:30
  51.7 0.3 collective-permute-start
  52.0 2.7 %collective-permute-start.11 = (f32[4,48,128]{2,1,0:T(8,128)S(1)}, f32[4,48,128]{2,1,0:T(8,128)S(1)}, u32[]{:S(2)}, u32[]{:S(2)}) collective-permute-start(f32[4,48,128]{2,1,0:T(8,128)S(1)} %pad_maximum_fusion.1.refs_0_), channel_id=1, source_target_pairs={{0,24},{4,28},{8,16},{12,20},{16,8},{20,12},{24,0},{28,4},{1,25},{... | collective-permute-start | bytes 294920 | tf_op jit(solution)/shard_map/ppermute | solution.py:30
  54.7 0.6 collective-permute-start.9
  55.3 2.4 %collective-permute-done.11.refs_6_ = f32[4,48,128]{2,1,0:T(8,128)S(1)} collective-permute-done((f32[4,48,128]{2,1,0:T(8,128)S(1)}, f32[4,48,128]{2,1,0:T(8,128)S(1)}, u32[]{:S(2)}, u32[]{:S(2)}) %collective-permute-start.11) | collective-permute-done | bytes 98336 | tf_op jit(solution)/shard_map/ppermute | solution.py:30
  57.7 1.7 %collective-permute-start.7 = (f32[4,48,128]{2,1,0:T(8,128)S(1)}, f32[4,48,128]{2,1,0:T(8,128)S(1)}, u32[]{:S(2)}, u32[]{:S(2)}) collective-permute-start(f32[4,48,128]{2,1,0:T(8,128)S(1)} %pad_maximum_fusion.1.refs_0_), channel_id=1, source_target_pairs={{0,8},{4,12},{8,0},{12,4},{16,24},{20,28},{24,16},{28,20},{1,9},{5... | collective-permute-start | bytes 294920 | tf_op jit(solution)/shard_map/ppermute | solution.py:30
  59.3 0.3 collective-permute-done.9.refs_4_
  59.7 2.6 %collective-permute-done.7.refs_2_ = f32[4,48,128]{2,1,0:T(8,128)S(1)} collective-permute-done((f32[4,48,128]{2,1,0:T(8,128)S(1)}, f32[4,48,128]{2,1,0:T(8,128)S(1)}, u32[]{:S(2)}, u32[]{:S(2)}) %collective-permute-start.7) | collective-permute-done | bytes 98336 | tf_op jit(solution)/shard_map/ppermute | solution.py:30
  62.3 0.6 copy-done.4
  62.9 0.5 collective-permute-start.10
  63.4 0.6 copy-done.6
  64.1 0.6 copy-done.8
  64.8 0.6 collective-permute-done.8.refs_3_
  65.4 0.9 copy-done.5
  66.3 0.9 copy-done.7
  67.1 0.9 copy-done.9
  68.0 1.0 assemble.1
  69.1 0.7 copy-done.1
  69.8 0.7 copy-done.3
  70.5 2.7 %gram_blocks.1 = f32[8,6,16,128]{3,2,1,0:T(8,128)S(1)} custom-call(s32[2]{0:T(128)S(1)} %pad_add_fusion.place, bf16[8192,128]{1,0:T(8,128)(2,1)S(1)} %copy-done, bf16[2048,128]{1,0:T(8,128)(2,1)} %collective-permute-done.rest_0_, bf16[2048,128]{1,0:T(8,128)(2,1)S(1)} %collective-permute-done.1.rest_1_, bf16[2048,128]{1,0:T(8,128)(2,1)S(1)} %collective-permute-done.2.rest_2_), custom_call_target="tpu_custom_call" | custom-call | tf_op jit(solution)/shard_map/gram_blocks/pallas_call | solution.py:77
  73.2 12.0 %all_to_all.10 = f32[8,6,16,128]{3,2,1,0:T(8,128)S(1)} all-to-all(f32[8,6,16,128]{3,2,1,0:T(8,128)S(1)} %gram_blocks.1), channel_id=1, replica_groups=mesh['term'=8,'topic'=4] {'term'}, dimensions={0} | all-to-all | bytes 786432 | tf_op jit(solution)/shard_map/all_to_all | solution.py:295
  85.2 2.9 %collective-permute-start.15 = (f32[6,16,128]{2,1,0:T(8,128)S(1)}, f32[6,16,128]{2,1,0:T(8,128)S(1)}, u32[]{:S(2)}, u32[]{:S(2)}) collective-permute-start(f32[6,16,128]{2,1,0:T(8,128)S(1)} %reduce_sum.19), channel_id=1, source_target_pairs={{0,3},{1,2},{2,1},{3,0},{4,7},{5,6},{6,5},{7,4},{8,11},{9,10},{10,... | collective-permute-start | bytes 147464 | tf_op jit(solution)/shard_map/ppermute | solution.py:30
  88.1 1.0 collective-permute-start.14
  89.1 0.6 collective-permute-start.13
  89.7 1.7 %collective-permute-done.15 = f32[6,16,128]{2,1,0:T(8,128)S(1)} collective-permute-done((f32[6,16,128]{2,1,0:T(8,128)S(1)}, f32[6,16,128]{2,1,0:T(8,128)S(1)}, u32[]{:S(2)}, u32[]{:S(2)}) %collective-permute-start.15) | collective-permute-done | bytes 49184 | tf_op jit(solution)/shard_map/ppermute | solution.py:30
  91.4 1.3 %collective-permute-done.14 = f32[6,16,128]{2,1,0:T(8,128)S(1)} collective-permute-done((f32[6,16,128]{2,1,0:T(8,128)S(1)}, f32[6,16,128]{2,1,0:T(8,128)S(1)}, u32[]{:S(2)}, u32[]{:S(2)}) %collective-permute-start.14) | collective-permute-done | bytes 49184 | tf_op jit(solution)/shard_map/ppermute | solution.py:30
  92.6 1.5 %collective-permute-done.13 = f32[6,16,128]{2,1,0:T(8,128)S(1)} collective-permute-done((f32[6,16,128]{2,1,0:T(8,128)S(1)}, f32[6,16,128]{2,1,0:T(8,128)S(1)}, u32[]{:S(2)}, u32[]{:S(2)}) %collective-permute-start.13) | collective-permute-done | bytes 49184 | tf_op jit(solution)/shard_map/ppermute | solution.py:30
  94.1 0.6 collective-permute-start.21
  94.8 1.5 %collective-permute-start.19 = (f32[6,16,128]{2,1,0:T(8,128)S(1)}, f32[6,16,128]{2,1,0:T(8,128)S(1)}, u32[]{:S(2)}, u32[]{:S(2)}) collective-permute-start(f32[6,16,128]{2,1,0:T(8,128)S(1)} %add_add_fusion.rest_0_), channel_id=1, source_target_pairs={{0,16},{4,20},{8,24},{12,28},{16,0},{20,4},{24,8},{28,12},{1,17},{... | collective-permute-start | bytes 147464 | tf_op jit(solution)/shard_map/ppermute | solution.py:30
  96.2 1.5 %collective-permute-start.17 = (f32[6,16,128]{2,1,0:T(8,128)S(1)}, f32[6,16,128]{2,1,0:T(8,128)S(1)}, u32[]{:S(2)}, u32[]{:S(2)}) collective-permute-start(f32[6,16,128]{2,1,0:T(8,128)S(1)} %add_add_fusion.rest_0_), channel_id=1, source_target_pairs={{0,8},{4,12},{8,0},{12,4},{16,24},{20,28},{24,16},{28,20},{1,9},{5... | collective-permute-start | bytes 147464 | tf_op jit(solution)/shard_map/ppermute | solution.py:30
  97.7 1.6 %collective-permute-done.21.rest_6_ = f32[6,16,128]{2,1,0:T(8,128)S(1)} collective-permute-done((f32[6,16,128]{2,1,0:T(8,128)S(1)}, f32[6,16,128]{2,1,0:T(8,128)S(1)}, u32[]{:S(2)}, u32[]{:S(2)}) %collective-permute-start.21) | collective-permute-done | bytes 49184 | tf_op jit(solution)/shard_map/ppermute | solution.py:30
  99.4 0.4 collective-permute-start.20
  99.8 0.5 collective-permute-done.17.rest_2_
  100.7 0.9 collective-permute-done.18.rest_3_
  101.5 0.9 copy-done.2
  102.5 7.6 %update.1 = (f32[16,128]{1,0:T(8,128)}, f32[64,128]{1,0:T(8,128)}, f32[8192,128]{1,0:T(8,128)}) custom-call(s32[2]{0:T(128)S(1)} %pad_add_fusion.place, s32[1,128]{1,0:T(1,128)S(1)} %copy-done.11, f32[4,128,128]{2,1,0:T(8,128)S(1)} %get-tuple-element.20.codes, f32[4,128,128]{2,1,0:T(8,128)S(1)} %copy-done.2, f32[4,128,128]{2,1,0:T(8,128)} %copy-done.3, ...), custom_call_target="tpu_custom_call" | custom-call | tf_op jit(solution)/shard_map/update/pallas_call | solution.py:218
  (44 shorter events, 1.1 us)
Async XLA Ops:
  0.6 3.1 %copy-start = (bf16[8192,128]{1,0:T(8,128)(2,1)S(1)}, bf16[8192,128]{1,0:T(8,128)(2,1)}, u32[]{:S(2)}) copy-start(bf16[8192,128]{1,0:T(8,128)(2,1)} %factor.1) | copy-start | bytes 6291460
  0.6 3.5 %copy-start.12 = (bf16[8192,128]{1,0:T(8,128)(2,1)S(1)}, bf16[8192,128]{1,0:T(8,128)(2,1)}, u32[]{:S(2)}) copy-start(bf16[8192,128]{1,0:T(8,128)(2,1)} %tiles.1) | copy-start | bytes 6291460
  4.1 0.8 copy-start.11
  4.1 12.3 %copy-start.13 = (f32[128,16]{0,1:T(8,128)S(1)}, f32[128,16]{0,1:T(8,128)}, u32[]{:S(2)}) copy-start(f32[128,16]{0,1:T(8,128)} %param.9) | copy-start | bytes 24580
  5.7 10.7 %all-to-all-start = ((f32[8,32,128]{2,1,0:T(8,128)}), f32[8,32,128]{2,1,0:T(8,128)S(1)}, u32[]{:S(2)}, u32[]{:S(2)}) async-start(f32[8,32,128]{2,1,0:T(8,128)} %pad_maximum_fusion), calls=%async_computation | async-start | bytes 262144 | tf_op jit(solution)/shard_map/all_to_all | solution.py:282
  11.8 58.7 %collective-permute-start.1 = (bf16[2048,128]{1,0:T(8,128)(2,1)}, bf16[2048,128]{1,0:T(8,128)(2,1)S(1)}, u32[]{:S(2)}, u32[]{:S(2)}) collective-permute-start(bf16[2048,128]{1,0:T(8,128)(2,1)} %constant_dynamic-slice_fusion.1), channel_id=1, source_target_pairs={{0,2},{1,3},{2,0},{3,1},{4,6},{5,7},{6,4},{7,5},{8,10},{9,11},{10,... | collective-permute-start | bytes 1572872 | tf_op jit(solution)/shard_map/ppermute | solution.py:30
  16.5 35.2 %collective-permute-start.4 = (f32[48,128]{1,0:T(8,128)S(1)}, f32[48,128]{1,0:T(8,128)S(1)}, u32[]{:S(2)}, u32[]{:S(2)}) collective-permute-start(f32[48,128]{1,0:T(8,128)S(1)} %get-tuple-element.32), channel_id=1, source_target_pairs={{0,2},{1,3},{2,0},{3,1},{4,6},{5,7},{6,4},{7,5},{8,10},{9,11},{10,... | collective-permute-start | bytes 73736 | tf_op jit(solution)/shard_map/ppermute | solution.py:30
  19.1 32.8 %collective-permute-start.3 = (f32[48,128]{1,0:T(8,128)S(1)}, f32[48,128]{1,0:T(8,128)S(1)}, u32[]{:S(2)}, u32[]{:S(2)}) collective-permute-start(f32[48,128]{1,0:T(8,128)S(1)} %get-tuple-element.32), channel_id=1, source_target_pairs={{0,1},{1,0},{2,3},{3,2},{4,5},{5,4},{6,7},{7,6},{8,9},{9,8},{10,11... | collective-permute-start | bytes 73736 | tf_op jit(solution)/shard_map/ppermute | solution.py:30
  20.7 31.3 %collective-permute-start.5 = (f32[48,128]{1,0:T(8,128)S(1)}, f32[48,128]{1,0:T(8,128)S(1)}, u32[]{:S(2)}, u32[]{:S(2)}) collective-permute-start(f32[48,128]{1,0:T(8,128)S(1)} %get-tuple-element.32), channel_id=1, source_target_pairs={{0,3},{1,2},{2,1},{3,0},{4,7},{5,6},{6,5},{7,4},{8,11},{9,10},{10,... | collective-permute-start | bytes 73736 | tf_op jit(solution)/shard_map/ppermute | solution.py:30
  22.0 48.5 %collective-permute-start.2 = (bf16[2048,128]{1,0:T(8,128)(2,1)}, bf16[2048,128]{1,0:T(8,128)(2,1)S(1)}, u32[]{:S(2)}, u32[]{:S(2)}) collective-permute-start(bf16[2048,128]{1,0:T(8,128)(2,1)} %get-tuple-element.29), channel_id=1, source_target_pairs={{0,3},{1,2},{2,1},{3,0},{4,7},{5,6},{6,5},{7,4},{8,11},{9,10},{10,... | collective-permute-start | bytes 1572872 | tf_op jit(solution)/shard_map/ppermute | solution.py:30
  51.7 18.8 %collective-permute-start = (bf16[2048,128]{1,0:T(8,128)(2,1)}, bf16[2048,128]{1,0:T(8,128)(2,1)}, u32[]{:S(2)}, u32[]{:S(2)}) collective-permute-start(bf16[2048,128]{1,0:T(8,128)(2,1)} %get-tuple-element.30), channel_id=1, source_target_pairs={{0,1},{1,0},{2,3},{3,2},{4,5},{5,4},{6,7},{7,6},{8,9},{9,8},{10,11... | collective-permute-start | bytes 1572872 | tf_op jit(solution)/shard_map/ppermute | solution.py:30
  52.0 5.7 %collective-permute-start.11 = (f32[4,48,128]{2,1,0:T(8,128)S(1)}, f32[4,48,128]{2,1,0:T(8,128)S(1)}, u32[]{:S(2)}, u32[]{:S(2)}) collective-permute-start(f32[4,48,128]{2,1,0:T(8,128)S(1)} %pad_maximum_fusion.1.refs_0_), channel_id=1, source_target_pairs={{0,24},{4,28},{8,16},{12,20},{16,8},{20,12},{24,0},{28,4},{1,25},{... | collective-permute-start | bytes 294920 | tf_op jit(solution)/shard_map/ppermute | solution.py:30
  54.7 4.9 %collective-permute-start.9 = (f32[4,48,128]{2,1,0:T(8,128)S(1)}, f32[4,48,128]{2,1,0:T(8,128)S(1)}, u32[]{:S(2)}, u32[]{:S(2)}) collective-permute-start(f32[4,48,128]{2,1,0:T(8,128)S(1)} %pad_maximum_fusion.1.refs_0_), channel_id=1, source_target_pairs={{0,16},{4,20},{8,24},{12,28},{16,0},{20,4},{24,8},{28,12},{1,17},{... | collective-permute-start | bytes 294920 | tf_op jit(solution)/shard_map/ppermute | solution.py:30
  57.7 4.6 %collective-permute-start.7 = (f32[4,48,128]{2,1,0:T(8,128)S(1)}, f32[4,48,128]{2,1,0:T(8,128)S(1)}, u32[]{:S(2)}, u32[]{:S(2)}) collective-permute-start(f32[4,48,128]{2,1,0:T(8,128)S(1)} %pad_maximum_fusion.1.refs_0_), channel_id=1, source_target_pairs={{0,8},{4,12},{8,0},{12,4},{16,24},{20,28},{24,16},{28,20},{1,9},{5... | collective-permute-start | bytes 294920 | tf_op jit(solution)/shard_map/ppermute | solution.py:30
  59.7 3.2 %collective-permute-start.6 = (f32[4,48,128]{2,1,0:T(8,128)S(1)}, f32[4,48,128]{2,1,0:T(8,128)}, u32[]{:S(2)}, u32[]{:S(2)}) collective-permute-start(f32[4,48,128]{2,1,0:T(8,128)S(1)} %pad_maximum_fusion.1.refs_0_), channel_id=1, source_target_pairs={{0,4},{4,0},{8,12},{12,8},{16,20},{20,16},{24,28},{28,24},{1,5},{5... | collective-permute-start | bytes 294920 | tf_op jit(solution)/shard_map/ppermute | solution.py:30
  62.3 1.8 %collective-permute-start.12 = (f32[4,48,128]{2,1,0:T(8,128)S(1)}, f32[4,48,128]{2,1,0:T(8,128)}, u32[]{:S(2)}, u32[]{:S(2)}) collective-permute-start(f32[4,48,128]{2,1,0:T(8,128)S(1)} %collective-permute-done.11.refs_6_), channel_id=1, source_target_pairs={{0,4},{4,0},{8,12},{12,8},{16,20},{20,16},{24,28},{28,24},{1,5},{5... | collective-permute-start | bytes 294920 | tf_op jit(solution)/shard_map/ppermute | solution.py:30
  62.3 0.6 copy-start.4
  62.9 1.9 %collective-permute-start.10 = (f32[4,48,128]{2,1,0:T(8,128)S(1)}, f32[4,48,128]{2,1,0:T(8,128)S(1)}, u32[]{:S(2)}, u32[]{:S(2)}) collective-permute-start(f32[4,48,128]{2,1,0:T(8,128)S(1)} %collective-permute-done.9.refs_4_), channel_id=1, source_target_pairs={{0,4},{4,0},{8,12},{12,8},{16,20},{20,16},{24,28},{28,24},{1,5},{5... | collective-permute-start | bytes 294920 | tf_op jit(solution)/shard_map/ppermute | solution.py:30
  63.4 0.6 copy-start.6
  64.1 1.3 %collective-permute-start.8 = (f32[4,48,128]{2,1,0:T(8,128)S(1)}, f32[4,48,128]{2,1,0:T(8,128)S(1)}, u32[]{:S(2)}, u32[]{:S(2)}) collective-permute-start(f32[4,48,128]{2,1,0:T(8,128)S(1)} %collective-permute-done.7.refs_2_), channel_id=1, source_target_pairs={{0,4},{4,0},{8,12},{12,8},{16,20},{20,16},{24,28},{28,24},{1,5},{5... | collective-permute-start | bytes 294920 | tf_op jit(solution)/shard_map/ppermute | solution.py:30
  64.1 0.6 copy-start.8
  65.4 0.9 copy-start.5
  66.2 0.9 copy-start.7
  67.1 0.9 copy-start.9
  69.1 0.7 copy-start.1
  69.8 0.7 copy-start.3
  70.5 31.0 %copy-start.10 = (f32[128,64]{0,1:T(8,128)S(1)}, f32[128,64]{0,1:T(8,128)}, u32[]{:S(2)}) copy-start(f32[128,64]{0,1:T(8,128)} %param.10) | copy-start | bytes 98308
  85.2 6.2 %collective-permute-start.15 = (f32[6,16,128]{2,1,0:T(8,128)S(1)}, f32[6,16,128]{2,1,0:T(8,128)S(1)}, u32[]{:S(2)}, u32[]{:S(2)}) collective-permute-start(f32[6,16,128]{2,1,0:T(8,128)S(1)} %reduce_sum.19), channel_id=1, source_target_pairs={{0,3},{1,2},{2,1},{3,0},{4,7},{5,6},{6,5},{7,4},{8,11},{9,10},{10,... | collective-permute-start | bytes 147464 | tf_op jit(solution)/shard_map/ppermute | solution.py:30
  88.1 4.5 %collective-permute-start.14 = (f32[6,16,128]{2,1,0:T(8,128)S(1)}, f32[6,16,128]{2,1,0:T(8,128)S(1)}, u32[]{:S(2)}, u32[]{:S(2)}) collective-permute-start(f32[6,16,128]{2,1,0:T(8,128)S(1)} %reduce_sum.19), channel_id=1, source_target_pairs={{0,1},{1,0},{2,3},{3,2},{4,5},{5,4},{6,7},{7,6},{8,9},{9,8},{10,11... | collective-permute-start | bytes 147464 | tf_op jit(solution)/shard_map/ppermute | solution.py:30
  89.1 5.0 %collective-permute-start.13 = (f32[6,16,128]{2,1,0:T(8,128)S(1)}, f32[6,16,128]{2,1,0:T(8,128)S(1)}, u32[]{:S(2)}, u32[]{:S(2)}) collective-permute-start(f32[6,16,128]{2,1,0:T(8,128)S(1)} %reduce_sum.19), channel_id=1, source_target_pairs={{0,2},{1,3},{2,0},{3,1},{4,6},{5,7},{6,4},{7,5},{8,10},{9,11},{10,... | collective-permute-start | bytes 147464 | tf_op jit(solution)/shard_map/ppermute | solution.py:30
  94.1 5.2 %collective-permute-start.21 = (f32[6,16,128]{2,1,0:T(8,128)S(1)}, f32[6,16,128]{2,1,0:T(8,128)S(1)}, u32[]{:S(2)}, u32[]{:S(2)}) collective-permute-start(f32[6,16,128]{2,1,0:T(8,128)S(1)} %add_add_fusion.rest_0_), channel_id=1, source_target_pairs={{0,24},{4,28},{8,16},{12,20},{16,8},{20,12},{24,0},{28,4},{1,25},{... | collective-permute-start | bytes 147464 | tf_op jit(solution)/shard_map/ppermute | solution.py:30
  94.8 4.6 %collective-permute-start.19 = (f32[6,16,128]{2,1,0:T(8,128)S(1)}, f32[6,16,128]{2,1,0:T(8,128)S(1)}, u32[]{:S(2)}, u32[]{:S(2)}) collective-permute-start(f32[6,16,128]{2,1,0:T(8,128)S(1)} %add_add_fusion.rest_0_), channel_id=1, source_target_pairs={{0,16},{4,20},{8,24},{12,28},{16,0},{20,4},{24,8},{28,12},{1,17},{... | collective-permute-start | bytes 147464 | tf_op jit(solution)/shard_map/ppermute | solution.py:30
  96.2 4.1 %collective-permute-start.17 = (f32[6,16,128]{2,1,0:T(8,128)S(1)}, f32[6,16,128]{2,1,0:T(8,128)S(1)}, u32[]{:S(2)}, u32[]{:S(2)}) collective-permute-start(f32[6,16,128]{2,1,0:T(8,128)S(1)} %add_add_fusion.rest_0_), channel_id=1, source_target_pairs={{0,8},{4,12},{8,0},{12,4},{16,24},{20,28},{24,16},{28,20},{1,9},{5... | collective-permute-start | bytes 147464 | tf_op jit(solution)/shard_map/ppermute | solution.py:30
  97.7 2.6 %collective-permute-start.16 = (f32[6,16,128]{2,1,0:T(8,128)S(1)}, f32[6,16,128]{2,1,0:T(8,128)S(1)}, u32[]{:S(2)}, u32[]{:S(2)}) collective-permute-start(f32[6,16,128]{2,1,0:T(8,128)S(1)} %add_add_fusion.rest_0_), channel_id=1, source_target_pairs={{0,4},{4,0},{8,12},{12,8},{16,20},{20,16},{24,28},{28,24},{1,5},{5... | collective-permute-start | bytes 147464 | tf_op jit(solution)/shard_map/ppermute | solution.py:30
  99.3 1.2 %collective-permute-start.22 = (f32[6,16,128]{2,1,0:T(8,128)S(1)}, f32[6,16,128]{2,1,0:T(8,128)S(1)}, u32[]{:S(2)}, u32[]{:S(2)}) collective-permute-start(f32[6,16,128]{2,1,0:T(8,128)S(1)} %collective-permute-done.21.rest_6_), channel_id=1, source_target_pairs={{0,4},{4,0},{8,12},{12,8},{16,20},{20,16},{24,28},{28,24},{1,5},{5... | collective-permute-start | bytes 147464 | tf_op jit(solution)/shard_map/ppermute | solution.py:30
  99.4 1.3 %collective-permute-start.20 = (f32[6,16,128]{2,1,0:T(8,128)S(1)}, f32[6,16,128]{2,1,0:T(8,128)S(1)}, u32[]{:S(2)}, u32[]{:S(2)}) collective-permute-start(f32[6,16,128]{2,1,0:T(8,128)S(1)} %collective-permute-done.19.rest_4_), channel_id=1, source_target_pairs={{0,4},{4,0},{8,12},{12,8},{16,20},{20,16},{24,28},{28,24},{1,5},{5... | collective-permute-start | bytes 147464 | tf_op jit(solution)/shard_map/ppermute | solution.py:30
  100.3 1.2 %collective-permute-start.18 = (f32[6,16,128]{2,1,0:T(8,128)S(1)}, f32[6,16,128]{2,1,0:T(8,128)S(1)}, u32[]{:S(2)}, u32[]{:S(2)}) collective-permute-start(f32[6,16,128]{2,1,0:T(8,128)S(1)} %collective-permute-done.17.rest_2_), channel_id=1, source_target_pairs={{0,4},{4,0},{8,12},{12,8},{16,20},{20,16},{24,28},{28,24},{1,5},{5... | collective-permute-start | bytes 147464 | tf_op jit(solution)/shard_map/ppermute | solution.py:30
  101.5 1.0 copy-start.2
where the time goes:
time: 111 us; the launch traced here: 110 us
  waiting for transfers between devices  42 us (38%)
  starting transfers between devices  30 us (27%)
  blocking collectives  12 us (11%)
  Pallas kernels  11.3 us (10%)
  local copies, waits for them, and re-layouts  9.12 us (8%)
  matrix products  4.05 us (4%)
    ppermute x23, waiting for transfers between devices, swap(): lax.ppermute(value, axis, [(i, i ^ offset) for i in range(lax.axis_size(a...  39.9 us
    ppermute x23, starting transfers between devices, swap(): lax.ppermute(value, axis, [(i, i ^ offset) for i in range(lax.axis_size(a...  24.8 us
    all_to_all x1, blocking collectives, per_device(): total = jnp.sum(lax.all_to_all(blocks, 'term', 0, 0, tiled=True), axis=0)  12 us
    pallas_call x1, Pallas kernels, update(): pl.pallas_call(functools.partial(update_kernel, devices, groups), out_sha...  7.57 us
    unnamed x28, local copies, waits for them, and re-layouts  7.26 us
    all_to_all x1, starting transfers between devices, per_device(): early = jnp.sum(lax.all_to_all(early, 'term', 0, 0, tiled=True), axis=0)  5.2 us
    dot_general x2, matrix products, contract_rows(): lax.dot_general(left, right, (((0,), (0,)), ((), ())), preferred_element_...  3.87 us
    pallas_call x1, Pallas kernels, gram_blocks(): pl.pallas_call(functools.partial(gram_kernel, groups), out_shape=jax.Shap...  2.69 us
  transfers between devices with their start and end apart: 24, of which 15 were waited for; matrix products, arithmetic and copies ran while one was open for 2% of the time, Pallas kernels for 1%

commit v1 on v0

--- a/solution.py
+++ b/solution.py
@@ -10,8 +10,8 @@
 ITERS = 3
 EPSILON = 1e-06
 DECAY = 0.5
-ROW_CHUNKS = 8
-UPDATE_GRANT = 53 * 2**20
+ROW_CHUNKS = 4
+UPDATE_GRANT = 48 * 2**20
 
 
 VMEM = pl.BlockSpec(memory_space=pltpu.VMEM)
@@ -47,46 +47,90 @@
     return [(i, j) for i in range(count) for j in range(i + 1, count)]
 
 
-def gram_kernel(groups, place, factor, *rest):
-    arrived = rest[: groups - 1]
-    out, rows, block, sem = rest[groups - 1 :]
+def load_rows(offsets, place, factor, arrived, rows, sem):
     z = place[0]
     share = rows.shape[1]
-    copies = [
-        pltpu.make_async_copy(
-            factor.at[pl.ds(pl.multiple_of(z * share, share), share)], rows.at[z], sem.at[0]
-        )
-    ]
-    for k in range(1, groups):
-        copies.append(pltpu.make_async_copy(arrived[k - 1], rows.at[z ^ k], sem.at[k]))
+    own = factor.at[pl.ds(pl.multiple_of(z * share, share), share)]
+    copies = [pltpu.make_async_copy(own, rows.at[z], sem.at[0])]
+    for index, (k, source) in enumerate(zip(offsets, arrived)):
+        copies.append(pltpu.make_async_copy(source, rows.at[z ^ k], sem.at[index + 1]))
     for copy in copies:
         copy.start()
     for copy in copies:
         copy.wait()
+
+
+def store_cut(out, index, block):
     devices, _, piece, _ = out.shape
+    for device in range(devices):
+        out[device, index] = block[device * piece : (device + 1) * piece, :]
+
+
+def first_pairs_kernel(groups, offsets, place, factor, *rest):
+    arrived = rest[: len(offsets)]
+    out, rows, sem = rest[len(offsets) :]
+    load_rows(offsets, place, factor, arrived, rows, sem)
+    last = place[2]
     for index, (i, j) in enumerate(pairs_of(groups)):
-        block[...] = contract_rows(rows[i], rows[j])
-        for device in range(devices):
-            out[device, index] = block[device * piece : (device + 1) * piece, :]
-
-
-def gram_blocks(place, factor, arrived, groups, devices):
+        waits = jnp.logical_or(last == i, last == j)
+
+        @pl.when(waits)
+        def _():
+            out[:, index] = jnp.zeros((out.shape[0],) + out.shape[2:], out.dtype)
+
+        @pl.when(jnp.logical_not(waits))
+        def _():
+            store_cut(out, index, contract_rows(rows[i], rows[j]))
+
+
+def last_pairs_kernel(groups, offsets, place, factor, *rest):
+    arrived = rest[: len(offsets)]
+    out, rows, sem = rest[len(offsets) :]
+    load_rows(offsets, place, factor, arrived, rows, sem)
+    last = place[2]
+    for k in range(1, groups):
+        other = last ^ k
+        left, right = jnp.minimum(last, other), jnp.maximum(last, other)
+        store_cut(out, k - 1, contract_rows(rows[left], rows[right]))
+
+
+def pair_products(kernel, count, place, factor, offsets, arrived, groups, devices):
     share, width = arrived[0].shape
-    shape = (devices, groups * (groups - 1) // 2, width // devices, width)
-    scratch = groups * share * width * 2 + groups * groups * width * width * 2
+    shape = (devices, count, width // devices, width)
+    grant = 4 * groups * share * width + 8 * devices * count * (width // devices) * width
     return pl.pallas_call(
-        functools.partial(gram_kernel, groups),
+        functools.partial(kernel, groups, offsets),
         out_shape=jax.ShapeDtypeStruct(shape, jnp.float32),
-        in_specs=[SMEM, ANY] + [ANY] * (groups - 1),
+        in_specs=[SMEM, ANY] + [ANY] * len(offsets),
         out_specs=VMEM,
         scratch_shapes=[
             pltpu.VMEM((groups, share, width), jnp.bfloat16),
-            pltpu.VMEM((width, width), jnp.float32),
             pltpu.SemaphoreType.DMA((groups,)),
         ],
-        compiler_params=pltpu.CompilerParams(vmem_limit_bytes=2 * scratch + 8 * 2**20),
-        name="gram_blocks",
+        compiler_params=pltpu.CompilerParams(vmem_limit_bytes=grant + 4 * 2**20),
     )(place, factor, *arrived)
+
+
+def merge_kernel(groups, place, first, last, out):
+    for index, (i, j) in enumerate(pairs_of(groups)):
+        waits = jnp.logical_or(place[2] == i, place[2] == j)
+        extra = last[0, (i ^ j) - 1]
+        for device in range(1, last.shape[0]):
+            extra = extra + last[device, (i ^ j) - 1]
+        out[index] = first[index] + jnp.where(waits, extra, 0.0)
+
+
+def merge(place, first, last, groups):
+    return pl.pallas_call(
+        functools.partial(merge_kernel, groups),
+        out_shape=jax.ShapeDtypeStruct(first.shape, jnp.float32),
+        in_specs=[SMEM, VMEM, VMEM],
+        out_specs=VMEM,
+        compiler_params=pltpu.CompilerParams(
+            vmem_limit_bytes=8 * (2 * first.size + last.size) + 2 * 2**20
+        ),
+        name="merge",
+    )(place, first, last)
 
 
 def assemble_kernel(devices, groups, place, *refs):
@@ -128,9 +172,7 @@
 def update_kernel(devices, groups, place, docs, codes, data, diagonal, stat, old, tiles, *rest):
     pieces = rest[:devices]
     codes_out, gram_new, data_new = rest[devices : devices + 3]
-    high, low, cur, blocks, tile_buf, old_buf, piece_sem, tile_sem, old_sem, new_sem = rest[
-        devices + 3 :
-    ]
+    high, low, cur, blocks, new, piece_sem, old_sem, new_sem = rest[devices + 3 :]
     z, term = place[0], place[1]
     width, documents = codes.shape[2], codes.shape[1]
     piece = width // devices
@@ -143,15 +185,13 @@
         copy.start()
         landings.append(copy)
     rows = old.shape[0] // ROW_CHUNKS
-    tile_in, old_in = [], []
-    for chunk in range(ROW_CHUNKS):
-        span = pl.ds(chunk * rows, rows)
-        copy = pltpu.make_async_copy(tiles.at[span], tile_buf.at[span], tile_sem.at[chunk])
+    spans = [pl.ds(chunk * rows, rows) for chunk in range(ROW_CHUNKS)]
+    loads = [
+        pltpu.make_async_copy(old.at[span], new.at[span], old_sem.at[chunk])
+        for chunk, span in enumerate(spans)
+    ]
+    for copy in loads:
         copy.start()
-        tile_in.append(copy)
-        copy = pltpu.make_async_copy(old.at[span], old_buf.at[span], old_sem.at[chunk])
-        copy.start()
-        old_in.append(copy)
     for copy in landings:
         copy.wait()
 
@@ -181,15 +221,13 @@
     picked = [contract_rows(onehot, value).astype(jnp.bfloat16) for value in own_pair]
     stacked = jnp.concatenate(picked, axis=0)
     stores = []
-    for chunk in range(ROW_CHUNKS):
-        span = pl.ds(chunk * rows, rows)
-        tile_in[chunk].wait()
-        old_in[chunk].wait()
-        tile = tile_buf[span, :]
-        old_buf[span, :] = DECAY * old_buf[span, :] + jnp.dot(
+    for chunk, span in enumerate(spans):
+        tile = tiles[span, :]
+        loads[chunk].wait()
+        new[span, :] = DECAY * new[span, :] + jnp.dot(
             jnp.concatenate([tile, tile], axis=1), stacked, preferred_element_type=jnp.float32
         )
-        copy = pltpu.make_async_copy(old_buf.at[span], data_new.at[span], new_sem.at[chunk])
+        copy = pltpu.make_async_copy(new.at[span], data_new.at[span], new_sem.at[chunk])
         copy.start()
         stores.append(copy)
 
@@ -222,17 +260,15 @@
             jax.ShapeDtypeStruct(stat.shape, jnp.float32),
             jax.ShapeDtypeStruct(old.shape, jnp.float32),
         ],
-        in_specs=[SMEM, VMEM, VMEM, VMEM, VMEM, VMEM, HBM, HBM] + [ANY] * devices,
+        in_specs=[SMEM, VMEM, VMEM, VMEM, VMEM, VMEM, HBM, VMEM] + [ANY] * devices,
         out_specs=[VMEM, VMEM, HBM],
         scratch_shapes=[
             pltpu.VMEM((topics, topics), jnp.bfloat16),
             pltpu.VMEM((topics, topics), jnp.bfloat16),
             pltpu.VMEM((documents, topics), jnp.float32),
             pltpu.VMEM((groups * (groups - 1) // 2, width, width), jnp.float32),
-            pltpu.VMEM(tiles.shape, tiles.dtype),
             pltpu.VMEM(old.shape, old.dtype),
             pltpu.SemaphoreType.DMA((devices,)),
-            pltpu.SemaphoreType.DMA((ROW_CHUNKS,)),
             pltpu.SemaphoreType.DMA((ROW_CHUNKS,)),
             pltpu.SemaphoreType.DMA((ROW_CHUNKS,)),
         ],
@@ -240,7 +276,11 @@
             vmem_limit_bytes=UPDATE_GRANT
         ),
         name="update",
-    )(place, docs, codes, data, diagonal, stat, old, tiles, *pieces)
+    )(
+        place, docs, codes, data, diagonal, stat,
+        old, tiles,
+        *pieces,
+    )
 
 
 def exchange_order(groups):
@@ -256,16 +296,14 @@
     mine = codes.shape[1]
     documents = mine * devices
     piece = width // devices
-    place = jnp.stack([z, term]).astype(jnp.int32)
-
     order = exchange_order(groups)
-    first, others = order[0], order[1:]
+    place = jnp.stack([z, term, z ^ order[-1]]).astype(jnp.int32)
 
     def exchange(k, source):
         block = lax.dynamic_slice_in_dim(source, (z ^ k) * share, share, 0)
         return swap(block, "topic", k)
 
-    arrived = {first: exchange(first, factor)}
+    arrived = {k: exchange(k, factor) for k in order[:-1]}
 
     onehot = (
         jnp.arange(documents, dtype=jnp.int32)[:, None] == tile_docs[0][None, :]
@@ -283,16 +321,24 @@
     early = jnp.concatenate([codes.T, early], axis=0)
     by_group = [early] + [swap(early, "topic", k) for k in range(1, groups)]
     later, early = lax.optimization_barrier((factor, early))
-    for k in others:
-        arrived[k] = exchange(k, later)
+    arrived[order[-1]] = exchange(order[-1], later)
     codes_all, data_all, diagonal_all = assemble(
         place, gather_term(jnp.stack(by_group), chips), documents
     )
-    arrived, codes_all, data_all, diagonal_all = lax.optimization_barrier(
-        (arrived, codes_all, data_all, diagonal_all)
-    )
-    blocks = gram_blocks(place, factor, [arrived[k] for k in range(1, groups)], groups, devices)
-    total = jnp.sum(lax.all_to_all(blocks, "term", 0, 0, tiled=True), axis=0)
+    blocks = pair_products(
+        first_pairs_kernel, groups * (groups - 1) // 2,
+        place, factor, order[:-1], [arrived[k] for k in order[:-1]], groups, devices,
+    )
+    first = jnp.sum(lax.all_to_all(blocks, "term", 0, 0, tiled=True), axis=0)
+    arrived, codes_all, data_all, diagonal_all, first = lax.optimization_barrier(
+        (arrived, codes_all, data_all, diagonal_all, first)
+    )
+
+    blocks = pair_products(
+        last_pairs_kernel, groups - 1,
+        place, factor, order, [arrived[k] for k in order], groups, devices,
+    )
+    total = merge(place, first, lax.all_to_all(blocks, "term", 0, 0, tiled=True), groups)
     whole = total
     for part in [swap(total, "topic", k) for k in order]:
         whole = whole + part

time: 111 us -> 110 us (level)
  local copies, waits for them, and re-layouts: 9.12 us -> 3.63 us
  starting transfers between devices: 30 us -> 34.3 us
  blocking collectives: 12 us -> 8.74 us
  waiting for transfers between devices: 42 us -> 43.9 us
  Pallas kernels: 11.3 us -> 12.8 us
    unnamed x28 -> x20, local copies, waits for them, and re-layouts: 7.26 us -> 1.77 us
    all_to_all x0 -> x1, starting transfers between devices: none -> 4.9 us  [per_device(): first = jnp.sum(lax.all_to_all(blocks, 'term', 0, 0, tiled=True), axis=0)]
    ppermute x23, waiting for transfers between devices: 39.9 us -> 43.6 us  [swap(): lax.ppermute(value, axis, [(i, i ^ offset) for i in range(lax.axis_size(a...]
    all_to_all x1, blocking collectives: 12 us -> 8.74 us  [per_device(): lax.all_to_all(blocks, 'term', 0, 0, tiled=True)]
    pallas_call x1 -> x3, Pallas kernels: 2.69 us -> 5.5 us  [the longest x2 4.94 us: pair_products(): pl.pallas_call(functools.partial(kernel, groups, offsets), out_shape=jax....]
    all_to_all x1, waiting for transfers between devices: 2.08 us -> 0.31 us  [per_device(): early = jnp.sum(lax.all_to_all(early, 'term', 0, 0, tiled=True), axis=0)]
  transfers between devices with their start and end apart: 24 -> 25, of which waited for: 15 -> 17; matrix products, arithmetic and copies ran while one was open for 2% -> 3% of each run, Pallas kernels for 1% -> 3%
where the time goes in v1:
time: 110 us
  waiting for transfers between devices  43.9 us (40%)
  starting transfers between devices  34.3 us (31%)
  Pallas kernels  12.8 us (12%)
  blocking collectives  8.74 us (8%)
  matrix products  4.05 us (4%)
  local copies, waits for them, and re-layouts  3.63 us (3%)
  other arithmetic  1.79 us (2%)
    ppermute x23, waiting for transfers between devices, swap(): lax.ppermute(value, axis, [(i, i ^ offset) for i in range(lax.axis_size(a...  43.6 us
    ppermute x23, starting transfers between devices, swap(): lax.ppermute(value, axis, [(i, i ^ offset) for i in range(lax.axis_size(a...  24.2 us
    all_to_all x1, blocking collectives, per_device(): lax.all_to_all(blocks, 'term', 0, 0, tiled=True)  8.74 us
    pallas_call x1, Pallas kernels, update(): pl.pallas_call(functools.partial(update_kernel, devices, groups), out_sha...  6.69 us
    all_to_all x1, starting transfers between devices, per_device(): early = jnp.sum(lax.all_to_all(early, 'term', 0, 0, tiled=True), axis=0)  5.2 us
    pallas_call x2, Pallas kernels, pair_products(): pl.pallas_call(functools.partial(kernel, groups, offsets), out_shape=jax....  4.94 us
    all_to_all x1, starting transfers between devices, per_device(): first = jnp.sum(lax.all_to_all(blocks, 'term', 0, 0, tiled=True), axis=0)  4.9 us
    dot_general x2, matrix products, contract_rows(): lax.dot_general(left, right, (((0,), (0,)), ((), ())), preferred_element_...  3.87 us
  transfers between devices with their start and end apart: 25, of which 17 were waited for; matrix products, arithmetic and copies ran while one was open for 3% of the time, Pallas kernels for 3%

profile of v1, /device:TPU:0, one launch (start us, length us, event | category | flops | bytes accessed | tf_op | source)
XLA Modules:
  0.0 110.1 jit_solution(14167692491527532449)
XLA Ops:
  0.7 3.1 %fusion.4 = f32[128,128]{1,0:T(8,128)S(1)} fusion(bf16[8192,128]{1,0:T(8,128)(2,1)} %factor.3), kind=kOutput, calls=%fused_computation.13 | convolution fusion | flops 268435456 | bytes 2162688 | tf_op jit(solution)/shard_map/dot_general | solution.py:24
  3.8 0.3 copy-done.1
  4.1 0.7 fusion.3
  4.9 0.2 fusion
  5.1 0.6 pad_maximum_fusion
  5.7 5.2 %all-to-all-start = ((f32[8,32,128]{2,1,0:T(8,128)}), f32[8,32,128]{2,1,0:T(8,128)S(1)}, u32[]{:S(2)}, u32[]{:S(2)}) async-start(f32[8,32,128]{2,1,0:T(8,128)} %pad_maximum_fusion), calls=%async_computation | async-start | bytes 262144 | tf_op jit(solution)/shard_map/all_to_all | solution.py:320
  10.9 1.0 constant_dynamic-slice_fusion.1
  12.0 2.6 %collective-permute-start.1 = (bf16[2048,128]{1,0:T(8,128)(2,1)}, bf16[2048,128]{1,0:T(8,128)(2,1)S(1)}, u32[]{:S(2)}, u32[]{:S(2)}) collective-permute-start(bf16[2048,128]{1,0:T(8,128)(2,1)} %get-tuple-element.31), channel_id=1, source_target_pairs={{0,2},{1,3},{2,0},{3,1},{4,6},{5,7},{6,4},{7,5},{8,10},{9,11},{10,... | collective-permute-start | bytes 1572872 | tf_op jit(solution)/shard_map/ppermute | solution.py:30
  14.5 1.6 %collective-permute-start = (bf16[2048,128]{1,0:T(8,128)(2,1)}, bf16[2048,128]{1,0:T(8,128)(2,1)S(1)}, u32[]{:S(2)}, u32[]{:S(2)}) collective-permute-start(bf16[2048,128]{1,0:T(8,128)(2,1)} %get-tuple-element.32), channel_id=1, source_target_pairs={{0,1},{1,0},{2,3},{3,2},{4,5},{5,4},{6,7},{7,6},{8,9},{9,8},{10,11... | collective-permute-start | bytes 1572872 | tf_op jit(solution)/shard_map/ppermute | solution.py:30
  16.1 0.3 all-to-all-done
  16.5 0.8 constant_dynamic-slice_fusion
  17.3 3.6 %collective-permute-start.2 = (bf16[2048,128]{1,0:T(8,128)(2,1)}, bf16[2048,128]{1,0:T(8,128)(2,1)}, u32[]{:S(2)}, u32[]{:S(2)}) collective-permute-start(bf16[2048,128]{1,0:T(8,128)(2,1)} %constant_dynamic-slice_fusion), channel_id=1, source_target_pairs={{0,3},{1,2},{2,1},{3,0},{4,7},{5,6},{6,5},{7,4},{8,11},{9,10},{10,... | collective-permute-start | bytes 1572872 | tf_op jit(solution)/shard_map/ppermute | solution.py:30
  21.0 18.2 %collective-permute-done.1.rest_0_ = bf16[2048,128]{1,0:T(8,128)(2,1)S(1)} collective-permute-done((bf16[2048,128]{1,0:T(8,128)(2,1)}, bf16[2048,128]{1,0:T(8,128)(2,1)S(1)}, u32[]{:S(2)}, u32[]{:S(2)}) %collective-permute-start.1) | collective-permute-done | bytes 524320 | tf_op jit(solution)/shard_map/ppermute | solution.py:30
  39.1 2.5 %shard_map.85 = f32[8,6,16,128]{3,2,1,0:T(8,128)} custom-call(s32[3]{0:T(128)S(1)} %pad_add_fusion.place, bf16[8192,128]{1,0:T(8,128)(2,1)S(1)} %copy-done, bf16[2048,128]{1,0:T(8,128)(2,1)S(1)} %collective-permute-done.1.rest_0_, bf16[2048,128]{1,0:T(8,128)(2,1)S(1)} %collective-permute-done.rest_1_), custom_call_target="tpu_custom_call" | custom-call | tf_op jit(solution)/shard_map/pallas_call | solution.py:101
  41.6 4.9 %all-to-all-start.1 = ((f32[8,6,16,128]{3,2,1,0:T(8,128)}), f32[8,6,16,128]{3,2,1,0:T(8,128)}, u32[]{:S(2)}, u32[]{:S(2)}) async-start(f32[8,6,16,128]{3,2,1,0:T(8,128)} %shard_map.85), calls=%async_computation.1 | async-start | bytes 786432 | tf_op jit(solution)/shard_map/all_to_all | solution.py:332
  46.5 0.9 collective-permute-start.4
  47.4 2.5 %collective-permute-start.3 = (f32[48,128]{1,0:T(8,128)S(1)}, f32[48,128]{1,0:T(8,128)S(1)}, u32[]{:S(2)}, u32[]{:S(2)}) collective-permute-start(f32[48,128]{1,0:T(8,128)S(1)} %get-tuple-element.34), channel_id=1, source_target_pairs={{0,1},{1,0},{2,3},{3,2},{4,5},{5,4},{6,7},{7,6},{8,9},{9,8},{10,11... | collective-permute-start | bytes 73736 | tf_op jit(solution)/shard_map/ppermute | solution.py:30
  50.0 1.0 collective-permute-start.5
  50.9 12.1 %collective-permute-done.4 = f32[48,128]{1,0:T(8,128)S(1)} collective-permute-done((f32[48,128]{1,0:T(8,128)S(1)}, f32[48,128]{1,0:T(8,128)S(1)}, u32[]{:S(2)}, u32[]{:S(2)}) %collective-permute-start.4) | collective-permute-done | bytes 24608 | tf_op jit(solution)/shard_map/ppermute | solution.py:30
  63.0 2.6 %collective-permute-start.11 = (f32[4,48,128]{2,1,0:T(8,128)S(1)}, f32[4,48,128]{2,1,0:T(8,128)S(1)}, u32[]{:S(2)}, u32[]{:S(2)}) collective-permute-start(f32[4,48,128]{2,1,0:T(8,128)S(1)} %pad_maximum_fusion.1.refs_0_), channel_id=1, source_target_pairs={{0,24},{4,28},{8,16},{12,20},{16,8},{20,12},{24,0},{28,4},{1,25},{... | collective-permute-start | bytes 294920 | tf_op jit(solution)/shard_map/ppermute | solution.py:30
  65.6 0.6 collective-permute-start.9
  66.2 0.4 collective-permute-start.7
  66.6 2.8 %collective-permute-done.11.refs_6_ = f32[4,48,128]{2,1,0:T(8,128)S(1)} collective-permute-done((f32[4,48,128]{2,1,0:T(8,128)S(1)}, f32[4,48,128]{2,1,0:T(8,128)S(1)}, u32[]{:S(2)}, u32[]{:S(2)}) %collective-permute-start.11) | collective-permute-done | bytes 98336 | tf_op jit(solution)/shard_map/ppermute | solution.py:30
  69.4 1.0 collective-permute-done.9.refs_4_
  70.3 0.5 collective-permute-done.7.refs_2_
  70.9 0.8 collective-permute-done.10.refs_5_
  71.6 0.5 collective-permute-done.8.refs_3_
  72.1 0.6 assemble.1
  72.7 0.7 copy-done.3
  73.5 0.7 copy-done.5
  74.2 1.0 reduce_sum.19.first
  75.2 2.5 %shard_map.86 = f32[8,3,16,128]{3,2,1,0:T(8,128)S(1)} custom-call(s32[3]{0:T(128)S(1)} %pad_add_fusion.place, bf16[8192,128]{1,0:T(8,128)(2,1)S(1)} %copy-done, bf16[2048,128]{1,0:T(8,128)(2,1)S(1)} %collective-permute-done.1.rest_0_, bf16[2048,128]{1,0:T(8,128)(2,1)S(1)} %collective-permute-done.rest_1_, bf16[2048,128]{1,0:T(8,128)(2,1)} %collective-permute-done.2.rest_2_), custom_call_target="tpu_custom_call" | custom-call | tf_op jit(solution)/shard_map/pallas_call | solution.py:101
  77.7 8.7 %all_to_all.15.last = f32[8,3,16,128]{3,2,1,0:T(8,128)S(1)} all-to-all(f32[8,3,16,128]{3,2,1,0:T(8,128)S(1)} %shard_map.86), channel_id=1, replica_groups=mesh['term'=8,'topic'=4] {'term'}, dimensions={0} | all-to-all | bytes 393216 | tf_op jit(solution)/shard_map/all_to_all | solution.py:341
  86.4 0.6 merge.1
  87.0 3.8 %collective-permute-start.15 = (f32[6,16,128]{2,1,0:T(8,128)S(1)}, f32[6,16,128]{2,1,0:T(8,128)S(1)}, u32[]{:S(2)}, u32[]{:S(2)}) collective-permute-start(f32[6,16,128]{2,1,0:T(8,128)S(1)} %merge.1), channel_id=1, source_target_pairs={{0,3},{1,2},{2,1},{3,0},{4,7},{5,6},{6,5},{7,4},{8,11},{9,10},{10,... | collective-permute-start | bytes 147464 | tf_op jit(solution)/shard_map/ppermute | solution.py:30
  90.9 0.5 collective-permute-start.13
  91.5 1.7 %collective-permute-done.15 = f32[6,16,128]{2,1,0:T(8,128)S(1)} collective-permute-done((f32[6,16,128]{2,1,0:T(8,128)S(1)}, f32[6,16,128]{2,1,0:T(8,128)S(1)}, u32[]{:S(2)}, u32[]{:S(2)}) %collective-permute-start.15) | collective-permute-done | bytes 49184 | tf_op jit(solution)/shard_map/ppermute | solution.py:30
  93.2 1.7 %collective-permute-done.14 = f32[6,16,128]{2,1,0:T(8,128)S(1)} collective-permute-done((f32[6,16,128]{2,1,0:T(8,128)S(1)}, f32[6,16,128]{2,1,0:T(8,128)S(1)}, u32[]{:S(2)}, u32[]{:S(2)}) %collective-permute-start.14) | collective-permute-done | bytes 49184 | tf_op jit(solution)/shard_map/ppermute | solution.py:30
  94.9 1.1 collective-permute-done.13
  95.9 0.6 collective-permute-start.21
  96.6 1.4 %collective-permute-start.19 = (f32[6,16,128]{2,1,0:T(8,128)S(1)}, f32[6,16,128]{2,1,0:T(8,128)S(1)}, u32[]{:S(2)}, u32[]{:S(2)}) collective-permute-start(f32[6,16,128]{2,1,0:T(8,128)S(1)} %add_add_fusion.rest_0_), channel_id=1, source_target_pairs={{0,16},{4,20},{8,24},{12,28},{16,0},{20,4},{24,8},{28,12},{1,17},{... | collective-permute-start | bytes 147464 | tf_op jit(solution)/shard_map/ppermute | solution.py:30
  98.0 1.5 %collective-permute-start.17 = (f32[6,16,128]{2,1,0:T(8,128)S(1)}, f32[6,16,128]{2,1,0:T(8,128)S(1)}, u32[]{:S(2)}, u32[]{:S(2)}) collective-permute-start(f32[6,16,128]{2,1,0:T(8,128)S(1)} %add_add_fusion.rest_0_), channel_id=1, source_target_pairs={{0,8},{4,12},{8,0},{12,4},{16,24},{20,28},{24,16},{28,20},{1,9},{5... | collective-permute-start | bytes 147464 | tf_op jit(solution)/shard_map/ppermute | solution.py:30
  99.5 1.6 %collective-permute-done.21.rest_6_ = f32[6,16,128]{2,1,0:T(8,128)S(1)} collective-permute-done((f32[6,16,128]{2,1,0:T(8,128)S(1)}, f32[6,16,128]{2,1,0:T(8,128)S(1)}, u32[]{:S(2)}, u32[]{:S(2)}) %collective-permute-start.21) | collective-permute-done | bytes 49184 | tf_op jit(solution)/shard_map/ppermute | solution.py:30
  101.2 0.4 collective-permute-start.20
  101.6 0.5 collective-permute-done.17.rest_2_
  102.1 0.2 collective-permute-done.22.rest_7_
  102.5 0.9 collective-permute-done.18.rest_3_
  103.4 6.7 %update.1 = (f32[16,128]{1,0:T(8,128)}, f32[64,128]{1,0:T(8,128)}, f32[8192,128]{1,0:T(8,128)}) custom-call(s32[3]{0:T(128)S(1)} %pad_add_fusion.place, s32[1,128]{1,0:T(1,128)S(1)} %copy-done.8, f32[4,128,128]{2,1,0:T(8,128)S(1)} %get-tuple-element.21.codes, f32[4,128,128]{2,1,0:T(8,128)S(1)} %copy-done.4, f32[4,128,128]{2,1,0:T(8,128)S(1)} %copy-done.6, ...), custom_call_target="tpu_custom_call" | custom-call | tf_op jit(solution)/shard_map/update/pallas_call | solution.py:256
  (40 shorter events, 0.7 us)
Async XLA Ops:
  0.6 3.1 %copy-start = (bf16[8192,128]{1,0:T(8,128)(2,1)S(1)}, bf16[8192,128]{1,0:T(8,128)(2,1)}, u32[]{:S(2)}) copy-start(bf16[8192,128]{1,0:T(8,128)(2,1)} %factor.3) | copy-start | bytes 6291460
  0.6 3.5 %copy-start.1 = (bf16[8192,128]{1,0:T(8,128)(2,1)S(1)}, bf16[8192,128]{1,0:T(8,128)(2,1)}, u32[]{:S(2)}) copy-start(bf16[8192,128]{1,0:T(8,128)(2,1)} %tiles.1) | copy-start | bytes 6291460
  4.1 0.8 copy-start.8
  4.9 11.6 %copy-start.9 = (f32[128,16]{0,1:T(8,128)S(1)}, f32[128,16]{0,1:T(8,128)}, u32[]{:S(2)}) copy-start(f32[128,16]{0,1:T(8,128)} %param.9) | copy-start | bytes 24580
  5.7 10.7 %all-to-all-start = ((f32[8,32,128]{2,1,0:T(8,128)}), f32[8,32,128]{2,1,0:T(8,128)S(1)}, u32[]{:S(2)}, u32[]{:S(2)}) async-start(f32[8,32,128]{2,1,0:T(8,128)} %pad_maximum_fusion), calls=%async_computation | async-start | bytes 262144 | tf_op jit(solution)/shard_map/all_to_all | solution.py:320
  12.0 27.2 %collective-permute-start.1 = (bf16[2048,128]{1,0:T(8,128)(2,1)}, bf16[2048,128]{1,0:T(8,128)(2,1)S(1)}, u32[]{:S(2)}, u32[]{:S(2)}) collective-permute-start(bf16[2048,128]{1,0:T(8,128)(2,1)} %get-tuple-element.31), channel_id=1, source_target_pairs={{0,2},{1,3},{2,0},{3,1},{4,6},{5,7},{6,4},{7,5},{8,10},{9,11},{10,... | collective-permute-start | bytes 1572872 | tf_op jit(solution)/shard_map/ppermute | solution.py:30
  14.5 24.6 %collective-permute-start = (bf16[2048,128]{1,0:T(8,128)(2,1)}, bf16[2048,128]{1,0:T(8,128)(2,1)S(1)}, u32[]{:S(2)}, u32[]{:S(2)}) collective-permute-start(bf16[2048,128]{1,0:T(8,128)(2,1)} %get-tuple-element.32), channel_id=1, source_target_pairs={{0,1},{1,0},{2,3},{3,2},{4,5},{5,4},{6,7},{7,6},{8,9},{9,8},{10,11... | collective-permute-start | bytes 1572872 | tf_op jit(solution)/shard_map/ppermute | solution.py:30
  17.3 57.9 %collective-permute-start.2 = (bf16[2048,128]{1,0:T(8,128)(2,1)}, bf16[2048,128]{1,0:T(8,128)(2,1)}, u32[]{:S(2)}, u32[]{:S(2)}) collective-permute-start(bf16[2048,128]{1,0:T(8,128)(2,1)} %constant_dynamic-slice_fusion), channel_id=1, source_target_pairs={{0,3},{1,2},{2,1},{3,0},{4,7},{5,6},{6,5},{7,4},{8,11},{9,10},{10,... | collective-permute-start | bytes 1572872 | tf_op jit(solution)/shard_map/ppermute | solution.py:30
  41.6 32.5 %all-to-all-start.1 = ((f32[8,6,16,128]{3,2,1,0:T(8,128)}), f32[8,6,16,128]{3,2,1,0:T(8,128)}, u32[]{:S(2)}, u32[]{:S(2)}) async-start(f32[8,6,16,128]{3,2,1,0:T(8,128)} %shard_map.85), calls=%async_computation.1 | async-start | bytes 786432 | tf_op jit(solution)/shard_map/all_to_all | solution.py:332
  46.5 16.5 %collective-permute-start.4 = (f32[48,128]{1,0:T(8,128)S(1)}, f32[48,128]{1,0:T(8,128)S(1)}, u32[]{:S(2)}, u32[]{:S(2)}) collective-permute-start(f32[48,128]{1,0:T(8,128)S(1)} %get-tuple-element.34), channel_id=1, source_target_pairs={{0,2},{1,3},{2,0},{3,1},{4,6},{5,7},{6,4},{7,5},{8,10},{9,11},{10,... | collective-permute-start | bytes 73736 | tf_op jit(solution)/shard_map/ppermute | solution.py:30
  47.4 15.6 %collective-permute-start.3 = (f32[48,128]{1,0:T(8,128)S(1)}, f32[48,128]{1,0:T(8,128)S(1)}, u32[]{:S(2)}, u32[]{:S(2)}) collective-permute-start(f32[48,128]{1,0:T(8,128)S(1)} %get-tuple-element.34), channel_id=1, source_target_pairs={{0,1},{1,0},{2,3},{3,2},{4,5},{5,4},{6,7},{7,6},{8,9},{9,8},{10,11... | collective-permute-start | bytes 73736 | tf_op jit(solution)/shard_map/ppermute | solution.py:30
  50.0 13.0 %collective-permute-start.5 = (f32[48,128]{1,0:T(8,128)S(1)}, f32[48,128]{1,0:T(8,128)S(1)}, u32[]{:S(2)}, u32[]{:S(2)}) collective-permute-start(f32[48,128]{1,0:T(8,128)S(1)} %get-tuple-element.34), channel_id=1, source_target_pairs={{0,3},{1,2},{2,1},{3,0},{4,7},{5,6},{6,5},{7,4},{8,11},{9,10},{10,... | collective-permute-start | bytes 73736 | tf_op jit(solution)/shard_map/ppermute | solution.py:30
  63.0 6.4 %collective-permute-start.11 = (f32[4,48,128]{2,1,0:T(8,128)S(1)}, f32[4,48,128]{2,1,0:T(8,128)S(1)}, u32[]{:S(2)}, u32[]{:S(2)}) collective-permute-start(f32[4,48,128]{2,1,0:T(8,128)S(1)} %pad_maximum_fusion.1.refs_0_), channel_id=1, source_target_pairs={{0,24},{4,28},{8,16},{12,20},{16,8},{20,12},{24,0},{28,4},{1,25},{... | collective-permute-start | bytes 294920 | tf_op jit(solution)/shard_map/ppermute | solution.py:30
  65.6 4.7 %collective-permute-start.9 = (f32[4,48,128]{2,1,0:T(8,128)S(1)}, f32[4,48,128]{2,1,0:T(8,128)S(1)}, u32[]{:S(2)}, u32[]{:S(2)}) collective-permute-start(f32[4,48,128]{2,1,0:T(8,128)S(1)} %pad_maximum_fusion.1.refs_0_), channel_id=1, source_target_pairs={{0,16},{4,20},{8,24},{12,28},{16,0},{20,4},{24,8},{28,12},{1,17},{... | collective-permute-start | bytes 294920 | tf_op jit(solution)/shard_map/ppermute | solution.py:30
  66.2 4.6 %collective-permute-start.7 = (f32[4,48,128]{2,1,0:T(8,128)S(1)}, f32[4,48,128]{2,1,0:T(8,128)S(1)}, u32[]{:S(2)}, u32[]{:S(2)}) collective-permute-start(f32[4,48,128]{2,1,0:T(8,128)S(1)} %pad_maximum_fusion.1.refs_0_), channel_id=1, source_target_pairs={{0,8},{4,12},{8,0},{12,4},{16,24},{20,28},{24,16},{28,20},{1,9},{5... | collective-permute-start | bytes 294920 | tf_op jit(solution)/shard_map/ppermute | solution.py:30
  66.6 4.3 %collective-permute-start.6 = (f32[4,48,128]{2,1,0:T(8,128)S(1)}, f32[4,48,128]{2,1,0:T(8,128)S(1)}, u32[]{:S(2)}, u32[]{:S(2)}) collective-permute-start(f32[4,48,128]{2,1,0:T(8,128)S(1)} %pad_maximum_fusion.1.refs_0_), channel_id=1, source_target_pairs={{0,4},{4,0},{8,12},{12,8},{16,20},{20,16},{24,28},{28,24},{1,5},{5... | collective-permute-start | bytes 294920 | tf_op jit(solution)/shard_map/ppermute | solution.py:30
  69.4 1.5 %collective-permute-start.12 = (f32[4,48,128]{2,1,0:T(8,128)S(1)}, f32[4,48,128]{2,1,0:T(8,128)S(1)}, u32[]{:S(2)}, u32[]{:S(2)}) collective-permute-start(f32[4,48,128]{2,1,0:T(8,128)S(1)} %collective-permute-done.11.refs_6_), channel_id=1, source_target_pairs={{0,4},{4,0},{8,12},{12,8},{16,20},{20,16},{24,28},{28,24},{1,5},{5... | collective-permute-start | bytes 294920 | tf_op jit(solution)/shard_map/ppermute | solution.py:30
  70.3 1.3 %collective-permute-start.10 = (f32[4,48,128]{2,1,0:T(8,128)S(1)}, f32[4,48,128]{2,1,0:T(8,128)S(1)}, u32[]{:S(2)}, u32[]{:S(2)}) collective-permute-start(f32[4,48,128]{2,1,0:T(8,128)S(1)} %collective-permute-done.9.refs_4_), channel_id=1, source_target_pairs={{0,4},{4,0},{8,12},{12,8},{16,20},{20,16},{24,28},{28,24},{1,5},{5... | collective-permute-start | bytes 294920 | tf_op jit(solution)/shard_map/ppermute | solution.py:30
  70.8 1.3 %collective-permute-start.8 = (f32[4,48,128]{2,1,0:T(8,128)S(1)}, f32[4,48,128]{2,1,0:T(8,128)S(1)}, u32[]{:S(2)}, u32[]{:S(2)}) collective-permute-start(f32[4,48,128]{2,1,0:T(8,128)S(1)} %collective-permute-done.7.refs_2_), channel_id=1, source_target_pairs={{0,4},{4,0},{8,12},{12,8},{16,20},{20,16},{24,28},{28,24},{1,5},{5... | collective-permute-start | bytes 294920 | tf_op jit(solution)/shard_map/ppermute | solution.py:30
  72.7 0.7 copy-start.3
  73.5 0.7 copy-start.5
  75.2 28.2 %copy-start.2 = (bf16[8192,128]{1,0:T(8,128)(2,1)S(1)}, bf16[8192,128]{1,0:T(8,128)(2,1)}, u32[]{:S(2)}) copy-start(bf16[8192,128]{1,0:T(8,128)(2,1)} %tiles.1) | copy-start | bytes 6291460
  75.2 28.2 %copy-start.4 = (f32[4,128,128]{2,1,0:T(8,128)S(1)}, f32[4,128,128]{2,1,0:T(8,128)}, u32[]{:S(2)}) copy-start(f32[4,128,128]{2,1,0:T(8,128)} %copy-done.3) | copy-start | bytes 786436
  75.2 28.1 %copy-start.6 = (f32[4,128,128]{2,1,0:T(8,128)S(1)}, f32[4,128,128]{2,1,0:T(8,128)}, u32[]{:S(2)}) copy-start(f32[4,128,128]{2,1,0:T(8,128)} %copy-done.5) | copy-start | bytes 786436
  75.2 28.1 %copy-start.7 = (f32[128,64]{0,1:T(8,128)S(1)}, f32[128,64]{0,1:T(8,128)}, u32[]{:S(2)}) copy-start(f32[128,64]{0,1:T(8,128)} %param.10) | copy-start | bytes 98308
  87.0 6.2 %collective-permute-start.15 = (f32[6,16,128]{2,1,0:T(8,128)S(1)}, f32[6,16,128]{2,1,0:T(8,128)S(1)}, u32[]{:S(2)}, u32[]{:S(2)}) collective-permute-start(f32[6,16,128]{2,1,0:T(8,128)S(1)} %merge.1), channel_id=1, source_target_pairs={{0,3},{1,2},{2,1},{3,0},{4,7},{5,6},{6,5},{7,4},{8,11},{9,10},{10,... | collective-permute-start | bytes 147464 | tf_op jit(solution)/shard_map/ppermute | solution.py:30
  90.8 4.1 %collective-permute-start.14 = (f32[6,16,128]{2,1,0:T(8,128)S(1)}, f32[6,16,128]{2,1,0:T(8,128)S(1)}, u32[]{:S(2)}, u32[]{:S(2)}) collective-permute-start(f32[6,16,128]{2,1,0:T(8,128)S(1)} %merge.1), channel_id=1, source_target_pairs={{0,1},{1,0},{2,3},{3,2},{4,5},{5,4},{6,7},{7,6},{8,9},{9,8},{10,11... | collective-permute-start | bytes 147464 | tf_op jit(solution)/shard_map/ppermute | solution.py:30
  90.9 5.0 %collective-permute-start.13 = (f32[6,16,128]{2,1,0:T(8,128)S(1)}, f32[6,16,128]{2,1,0:T(8,128)S(1)}, u32[]{:S(2)}, u32[]{:S(2)}) collective-permute-start(f32[6,16,128]{2,1,0:T(8,128)S(1)} %merge.1), channel_id=1, source_target_pairs={{0,2},{1,3},{2,0},{3,1},{4,6},{5,7},{6,4},{7,5},{8,10},{9,11},{10,... | collective-permute-start | bytes 147464 | tf_op jit(solution)/shard_map/ppermute | solution.py:30
  95.9 5.2 %collective-permute-start.21 = (f32[6,16,128]{2,1,0:T(8,128)S(1)}, f32[6,16,128]{2,1,0:T(8,128)S(1)}, u32[]{:S(2)}, u32[]{:S(2)}) collective-permute-start(f32[6,16,128]{2,1,0:T(8,128)S(1)} %add_add_fusion.rest_0_), channel_id=1, source_target_pairs={{0,24},{4,28},{8,16},{12,20},{16,8},{20,12},{24,0},{28,4},{1,25},{... | collective-permute-start | bytes 147464 | tf_op jit(solution)/shard_map/ppermute | solution.py:30
  96.6 4.6 %collective-permute-start.19 = (f32[6,16,128]{2,1,0:T(8,128)S(1)}, f32[6,16,128]{2,1,0:T(8,128)S(1)}, u32[]{:S(2)}, u32[]{:S(2)}) collective-permute-start(f32[6,16,128]{2,1,0:T(8,128)S(1)} %add_add_fusion.rest_0_), channel_id=1, source_target_pairs={{0,16},{4,20},{8,24},{12,28},{16,0},{20,4},{24,8},{28,12},{1,17},{... | collective-permute-start | bytes 147464 | tf_op jit(solution)/shard_map/ppermute | solution.py:30
  98.0 4.1 %collective-permute-start.17 = (f32[6,16,128]{2,1,0:T(8,128)S(1)}, f32[6,16,128]{2,1,0:T(8,128)S(1)}, u32[]{:S(2)}, u32[]{:S(2)}) collective-permute-start(f32[6,16,128]{2,1,0:T(8,128)S(1)} %add_add_fusion.rest_0_), channel_id=1, source_target_pairs={{0,8},{4,12},{8,0},{12,4},{16,24},{20,28},{24,16},{28,20},{1,9},{5... | collective-permute-start | bytes 147464 | tf_op jit(solution)/shard_map/ppermute | solution.py:30
  99.5 2.6 %collective-permute-start.16 = (f32[6,16,128]{2,1,0:T(8,128)S(1)}, f32[6,16,128]{2,1,0:T(8,128)S(1)}, u32[]{:S(2)}, u32[]{:S(2)}) collective-permute-start(f32[6,16,128]{2,1,0:T(8,128)S(1)} %add_add_fusion.rest_0_), channel_id=1, source_target_pairs={{0,4},{4,0},{8,12},{12,8},{16,20},{20,16},{24,28},{28,24},{1,5},{5... | collective-permute-start | bytes 147464 | tf_op jit(solution)/shard_map/ppermute | solution.py:30
  101.1 1.2 %collective-permute-start.22 = (f32[6,16,128]{2,1,0:T(8,128)S(1)}, f32[6,16,128]{2,1,0:T(8,128)S(1)}, u32[]{:S(2)}, u32[]{:S(2)}) collective-permute-start(f32[6,16,128]{2,1,0:T(8,128)S(1)} %collective-permute-done.21.rest_6_), channel_id=1, source_target_pairs={{0,4},{4,0},{8,12},{12,8},{16,20},{20,16},{24,28},{28,24},{1,5},{5... | collective-permute-start | bytes 147464 | tf_op jit(solution)/shard_map/ppermute | solution.py:30
  101.2 1.3 %collective-permute-start.20 = (f32[6,16,128]{2,1,0:T(8,128)S(1)}, f32[6,16,128]{2,1,0:T(8,128)S(1)}, u32[]{:S(2)}, u32[]{:S(2)}) collective-permute-start(f32[6,16,128]{2,1,0:T(8,128)S(1)} %collective-permute-done.19.rest_4_), channel_id=1, source_target_pairs={{0,4},{4,0},{8,12},{12,8},{16,20},{20,16},{24,28},{28,24},{1,5},{5... | collective-permute-start | bytes 147464 | tf_op jit(solution)/shard_map/ppermute | solution.py:30
  102.1 1.2 %collective-permute-start.18 = (f32[6,16,128]{2,1,0:T(8,128)S(1)}, f32[6,16,128]{2,1,0:T(8,128)S(1)}, u32[]{:S(2)}, u32[]{:S(2)}) collective-permute-start(f32[6,16,128]{2,1,0:T(8,128)S(1)} %collective-permute-done.17.rest_2_), channel_id=1, source_target_pairs={{0,4},{4,0},{8,12},{12,8},{16,20},{20,16},{24,28},{28,24},{1,5},{5... | collective-permute-start | bytes 147464 | tf_op jit(solution)/shard_map/ppermute | solution.py:30
